TPU v7x, 512 devices: a whole 4x4x16 slice. The times are simulated.
512 devices in a mesh: req: 128 (over z_hi, y, x, core), tp: 4 (over z_lo).
Axes of the slice: x: 4, y: 4, z: 16 (z_hi: 4, z_lo: 4; z = z_hi * 4 + z_lo), core: 2. Of those that a mesh axis runs over, the one named last changes fastest.
Arguments:
- queries: bfloat16 [8192, 2560], P('req', 'tp'), may hold values from -20 to 20
- key_values: bfloat16 [8192, 1024], P('req', 'tp'), may hold values from -6 to 6
- hidden: bfloat16 [8192, 2560], P('req'), may hold values from -6 to 6
- lengths: int32 [128, 4], P('req'), may hold values from 1 to 32, 64 in all within a row
- page_table: int32 [128, 4, 2], P('req'), may hold values from 0 to 7, as said below
- out_weight: bfloat16 [2560, 2560], P('tp', 'req'), may hold values from -0.125 to 0.125
- norm_gain: float32 [2560], replicated, may hold values from 0.4 to 1.6
- expert_choice: int32 [8192, 6], P('req'), may hold values from 0 to 63, all different within a row; in each aligned block of 64 rows (0 to 63, 64 to 127, ...) at most 8 rows name the same one
- route_weight: float32 [8192, 6], P('req'), may hold values from 0.05 to 0.5
- gate_up: bfloat16 [128, 2560, 1536], P('req', None, 'tp'), may hold values from -0.125 to 0.125
- down: bfloat16 [128, 768, 2560], P('req', 'tp'), may hold values from -0.15625 to 0.15625
Outputs:
- layer_out: bfloat16 [8192, 2560], P('req', 'tp')
- kv_cache: bfloat16 [1024, 16, 1024], P('req', None, 'tp')
Inputs may be any that keep to these rules, and one draw needn't show every extreme that they name: `expert_choice`: among the 64 rows of one index of req no expert is named by more than 8 rows; the 6 experts of a row differ. `page_table`: the 4 x 2 entries of one index of req are its 8 pool pages, each once.
All inputs are finite; a program needn't handle non-finite values.
Results may differ from a plain program's by a relative error of at most 0.0065.
Values may be sent and summed in bfloat16 or wider, within the bound.
No kernel may reach another device: no remote copies, remote signals or barrier semaphores. Data moves between devices by JAX's collectives and lax.ppermute only.
A program may use at most 64 MiB of HBM per device.

v0:
```python
import jax
import jax.numpy as jnp
from jax import lax
from jax.sharding import PartitionSpec as P

HEAD_DIM = 128
PAGE = 16
epsilon = 1e-05


def prompt_layout(lengths, count):
    ends = jnp.cumsum(lengths)
    starts = ends - lengths
    places = jnp.arange(count, dtype=jnp.int32)
    segment = jnp.sum((ends[None, :] <= places[:, None]).astype(jnp.int32), axis=1)
    picked = segment[:, None] == jnp.arange(lengths.shape[0], dtype=jnp.int32)[None, :]
    offset = places - jnp.sum(jnp.where(picked, starts[None, :], 0), axis=1)
    return (segment, offset)


def attend(queries, key_values, segment):
    count = queries.shape[0]
    local_kv = key_values.shape[1] // (2 * HEAD_DIM)
    local_heads = queries.shape[1] // HEAD_DIM
    group = local_heads // local_kv
    query_rows = queries.reshape(count, local_kv, group, HEAD_DIM)
    key_rows = key_values.reshape(count, local_kv, 2, HEAD_DIM)
    scores = jnp.einsum(
        "qhgd,khd->hgqk", query_rows, key_rows[:, :, 0], preferred_element_type=jnp.float32
    ) * HEAD_DIM ** (-0.5)
    places = jnp.arange(count, dtype=jnp.int32)
    allowed = (segment[:, None] == segment[None, :]) & (places[None, :] <= places[:, None])
    scores = jnp.where(allowed[None, None], scores, -1e30)
    highest = jnp.max(scores, axis=-1, keepdims=True)
    weights = jnp.exp(scores - highest)
    probs = (weights / jnp.sum(weights, axis=-1, keepdims=True)).astype(jnp.bfloat16)
    context = jnp.einsum(
        "hgqk,khd->qhgd", probs, key_rows[:, :, 1], preferred_element_type=jnp.float32
    )
    return context.astype(jnp.bfloat16).reshape(count, local_heads * HEAD_DIM)


def on_device(
    queries,
    key_values,
    hidden,
    lengths,
    page_table,
    out_weight,
    norm_gain,
    expert_choice,
    route_weight,
    gate_up,
    down,
):
    count = queries.shape[0]
    width = hidden.shape[1]
    share = width // lax.axis_size("tp")
    own_start = lax.axis_index("tp") * share
    segment, offset = prompt_layout(lengths[0], count)
    context = attend(queries, key_values, segment)
    attn_part = jnp.dot(
        context,
        lax.all_gather(out_weight, "req", axis=1, tiled=True),
        preferred_element_type=jnp.float32,
    )
    attn = lax.psum(attn_part, "tp")
    mid_full = (hidden.astype(jnp.float32) + attn).astype(jnp.bfloat16)
    mid_wide = lax.optimization_barrier(mid_full).astype(jnp.float32)
    square = jnp.mean(mid_wide * mid_wide, axis=1, keepdims=True)
    normed = (mid_wide * lax.rsqrt(square + epsilon) * norm_gain).astype(jnp.bfloat16)
    mid_own = lax.dynamic_slice_in_dim(mid_wide, own_start, share, 1)
    chosen_count = expert_choice.shape[1]
    experts = lax.axis_size("req") // 2
    capacity = 2 * ((count * chosen_count * 2 + 3 * experts - 1) // (3 * experts))
    flat_choice = expert_choice.reshape(-1)
    hits = (flat_choice[:, None] == jnp.arange(experts, dtype=jnp.int32)[None, :]).astype(jnp.int32)
    ranks = jnp.sum((jnp.cumsum(hits, axis=0) - hits) * hits, axis=1)
    target = flat_choice * capacity + ranks
    onehot = (target[:, None] == jnp.arange(experts * capacity, dtype=jnp.int32)[None, :]).astype(
        jnp.bfloat16
    )
    selector = jnp.sum(onehot.reshape(count, chosen_count, experts * capacity), axis=1)
    outgoing = jnp.dot(selector.T, normed, preferred_element_type=jnp.float32).astype(jnp.bfloat16)
    outgoing = outgoing.reshape(experts, capacity, normed.shape[1])
    gate_up_local = gate_up[0]
    down_local = down[0]
    units = down_local.shape[0]
    doubled = jnp.broadcast_to(outgoing[:, None], (experts, 2, capacity, outgoing.shape[2]))
    doubled = doubled.reshape(2 * experts, capacity, outgoing.shape[2])
    full_rows = lax.all_to_all(doubled, "req", split_axis=0, concat_axis=0, tiled=True)
    senders = full_rows.shape[0]
    items = full_rows.shape[1]
    projected = jnp.dot(
        full_rows.reshape(senders * items, width), gate_up_local, preferred_element_type=jnp.float32
    )
    activated = (jax.nn.silu(projected[:, :units]) * projected[:, units:]).astype(jnp.bfloat16)
    partial_value = jnp.dot(activated, down_local, preferred_element_type=jnp.float32).astype(
        jnp.bfloat16
    )
    incoming = lax.all_to_all(
        partial_value.reshape(senders, items, width), "req", split_axis=0, concat_axis=0, tiled=True
    )
    slot_out = jnp.sum(incoming.reshape(experts, 2, capacity, width).astype(jnp.float32), axis=1)
    slot_out = slot_out.reshape(experts * capacity, width)
    picked = jnp.take(slot_out, target, axis=0).reshape(count, chosen_count, width)
    moe_part = jnp.sum(picked * route_weight[:, :, None], axis=1)
    moe = lax.psum_scatter(
        moe_part.astype(jnp.bfloat16), "tp", scatter_dimension=1, tiled=True
    ).astype(jnp.float32)
    layer_out = (mid_own + moe).astype(jnp.bfloat16)
    pages = page_table[0]
    flat_pages = pages.reshape(-1)
    pool_pages = flat_pages.shape[0]
    page_of = segment * pages.shape[1] + offset // PAGE
    slot_page = jnp.sum(
        jnp.where(
            page_of[:, None] == jnp.arange(pool_pages, dtype=jnp.int32)[None, :],
            flat_pages[None, :],
            0,
        ),
        axis=1,
    )
    cache_rows = slot_page * PAGE + offset % PAGE
    cache = (
        jnp.zeros((pool_pages * PAGE, key_values.shape[1]), jnp.bfloat16)
        .at[cache_rows]
        .set(key_values)
    )
    return (layer_out, cache.reshape(pool_pages, PAGE, key_values.shape[1]))


def solution(mesh):
    placed = (
        P("req", "tp"),
        P("req", "tp"),
        P("req", None),
        P("req", None),
        P("req", None, None),
        P("tp", "req"),
        P(),
        P("req", None),
        P("req", None),
        P("req", None, "tp"),
        P("req", "tp", None),
    )
    return jax.shard_map(
        on_device,
        mesh=mesh,
        in_specs=placed,
        out_specs=(P("req", "tp"), P("req", None, "tp")),
        check_vma=False,
    )
```

profile of v0, /device:TPU:4, one launch (start us, length us, event | category | flops | bytes accessed | tf_op | source)
XLA Modules:
  0.0 765.0 jit_solution(7705690440970895287)
XLA Ops:
  7.2 0.0 copy-start
  7.2 0.0 all-gather.3.cloned.1.call-start
  7.2 0.7 all-gather.3.cloned.1.call-update
  7.9 0.0 all-reduce.2.cloned.1.call-start
  8.0 0.8 reshape.288
  8.7 0.8 reduce-window.10
  9.6 0.1 convert_reduce_fusion.1
  9.7 0.1 fusion.30
  9.8 1.1 fusion.41
  10.9 0.2 fusion.7
  11.2 0.1 copy.57
  11.2 0.8 copy.58
  12.0 0.1 eq.88
  12.1 0.0 copy-start.2
  12.2 0.0 copy-start.1
  12.2 117.9 %all-gather.3.cloned.1.call-done = bf16[128,20,640]{2,1,0:T(8,128)(2,1)} async-done(((bf16[1,20,640]{2,1,0:T(8,128)(2,1)}), bf16[128,20,640]{2,1,0:T(8,128)(2,1)}) %all-gather.3.cloned.1.call-update) | async-done | bytes 3276816 | tf_op jit(solution)/shard_map/all_gather | solution.py:64
  130.1 6.1 reshape.320
  136.2 0.0 copy-start.3
  136.2 3.9 fusion.22
  140.1 0.0 all-reduce.2.cloned.1.call-update
  140.2 0.1 reshape.294
  140.3 0.9 reduce-window.11
  141.2 0.2 slice_reduce_fusion
  141.5 0.1 fusion.20
  141.6 0.1 reduce_sum.93
  141.7 0.1 copy.61
  141.8 0.0 copy-done.2
  141.8 0.1 fusion.11
  142.0 56.9 %all-reduce.2.cloned.1.call-done = f32[64,2560]{1,0:T(8,128)} async-done(((f32[64,2560]{1,0:T(8,128)}), f32[64,2560]{1,0:T(8,128)}) %all-reduce.2.cloned.1.call-update) | async-done | bytes 655376 | tf_op jit(solution)/shard_map/psum | solution.py:67
  198.9 0.0 copy-done.1
  198.9 1.1 add_convert_fusion
  200.1 0.2 multiply_reduce_fusion.1
  200.2 0.0 copy-done.3
  200.3 0.9 fusion.3
  201.2 0.4 broadcast_in_dim.85
  201.6 253.4 %all_to_all.10 = bf16[128,8,2560]{2,1,0:T(8,128)(2,1)S(1)} all-to-all(bf16[128,8,2560]{2,1,0:T(8,128)(2,1)S(1)} %bitcast.109), channel_id=1, replica_groups=mesh['req'=128,'tp'=4] {'req'}, dimensions={0} | all-to-all | bytes 10485760 | tf_op jit(solution)/shard_map/all_to_all | solution.py:91
  454.9 0.0 copy-done
  454.9 2.2 fusion
  457.2 0.0 copy-done.6
  457.2 4.0 fusion.2
  461.1 9.4 %all-to-all-start.1 = ((bf16[128,8,2560]{2,1,0:T(8,128)(2,1)}), bf16[128,8,2560]{2,1,0:T(8,128)(2,1)}, u32[]{:S(2)}, u32[]{:S(2)}) async-start(bf16[128,8,2560]{2,1,0:T(8,128)(2,1)} %fusion.2), calls=%async_computation.1 | async-start | bytes 10485760 | tf_op jit(solution)/shard_map/all_to_all | solution.py:101
  470.6 0.2 reduce-scatter.4.cloned.1.call-start
  470.8 0.1 copy.63
  470.9 0.1 mul.113
  471.1 0.1 copy.62
  471.2 0.0 copy-done.4
  471.2 0.1 copy.64
  471.3 0.0 copy-done.5
  471.3 0.1 copy.65
  471.4 0.1 broadcast_in_dim.91
  471.5 0.0 copy-done.7
  471.5 194.3 %all-to-all-done.1 = bf16[128,8,2560]{2,1,0:T(8,128)(2,1)} async-done(((bf16[128,8,2560]{2,1,0:T(8,128)(2,1)}), bf16[128,8,2560]{2,1,0:T(8,128)(2,1)}, u32[]{:S(2)}, u32[]{:S(2)}) %all-to-all-start.1) | async-done | bytes 5242912 | tf_op jit(solution)/shard_map/all_to_all | solution.py:101
  665.8 6.2 convert_reduce_fusion
  672.0 8.4 %gather_fusion = f32[384,2560]{1,0:T(8,128)} fusion(f32[512,2560]{1,0:T(8,128)} %bitcast.108, s32[1024]{0:T(1024)S(1)} %pad_clamp_fusion), kind=kCustom, calls=%fused_computation | custom fusion | bytes 7865856 | tf_op jit(solution)/shard_map/jit(_take)/gather | solution.py:106
  680.4 5.1 gather.7
  685.5 4.7 multiply_reduce_fusion
  690.3 1.1 copy.67
  691.4 0.0 reduce-scatter.4.cloned.1.call-update
  691.4 0.1 select_reduce_fusion.1
  691.5 0.1 select_reduce_fusion
  691.6 1.6 scatter_custom_fusion
  693.3 63.5 %reduce-scatter.4.cloned.1.call-done = bf16[640,64]{1,0:T(8,128)(2,1)} async-done(((bf16[2560,64]{1,0:T(8,128)(2,1)}), bf16[640,64]{1,0:T(8,128)(2,1)}) %reduce-scatter.4.cloned.1.call-update) | async-done | bytes 81936
  756.8 1.0 copy.68
  757.8 0.7 add_convert_fusion.1
  (17 shorter events, 0.3 us)
Async XLA Ops:
  7.2 447.8 %copy-start = (bf16[1,2560,384]{2,1,0:T(8,128)(2,1)S(1)}, bf16[1,2560,384]{2,1,0:T(8,128)(2,1)}, u32[]{:S(2)}) copy-start(bf16[1,2560,384]{2,1,0:T(8,128)(2,1)} %param.20) | copy-start | bytes 5898244
  7.2 122.9 %all-gather.3.cloned.1.call-start = ((), (), s32[]{:S(2)}) async-start(), calls=%async_computation.4 | async-start | bytes 3962880 | tf_op jit(solution)/shard_map/all_gather | solution.py:64
  7.9 191.0 %all-reduce.2.cloned.1.call-start = ((), (), s32[]{:S(2)}) async-start(), calls=%async_computation.3 | async-start | bytes 1310720 | tf_op jit(solution)/shard_map/psum | solution.py:67
  12.1 129.7 %copy-start.2 = (s32[64,6]{0,1:T(8,128)S(1)}, s32[64,6]{0,1:T(8,128)}, u32[]{:S(2)}) copy-start(s32[64,6]{0,1:T(8,128)} %param.18) | copy-start | bytes 4612
  12.2 186.8 %copy-start.1 = (bf16[64,2560]{1,0:T(8,128)(2,1)S(1)}, bf16[64,2560]{1,0:T(8,128)(2,1)}, u32[]{:S(2)}) copy-start(bf16[64,2560]{1,0:T(8,128)(2,1)} %param.13) | copy-start | bytes 983044
  136.2 64.0 %copy-start.3 = (f32[2560]{0:T(1024)S(1)}, f32[2560]{0:T(1024)}, u32[]{:S(2)}) copy-start(f32[2560]{0:T(1024)} %param.17) | copy-start | bytes 30724
  454.9 2.2 copy-start.6
  461.1 10.0 %copy-start.4 = (f32[64,6]{0,1:T(8,128)S(1)}, f32[64,6]{0,1:T(8,128)}, u32[]{:S(2)}) copy-start(f32[64,6]{0,1:T(8,128)} %param.19) | copy-start | bytes 4612
  461.1 10.1 %copy-start.5 = (s32[1,4,2]{1,2,0:T(2,128)S(1)}, s32[1,4,2]{1,2,0:T(2,128)}, u32[]{:S(2)}) copy-start(s32[1,4,2]{1,2,0:T(2,128)} %param.15) | copy-start | bytes 100
  461.1 10.4 %copy-start.7 = (s32[1,4]{1,0:T(1,128)S(1)}, s32[1,4]{1,0:T(1,128)}, u32[]{:S(2)}) copy-start(s32[1,4]{1,0:T(1,128)} %param.14) | copy-start | bytes 52
  461.1 204.6 %all-to-all-start.1 = ((bf16[128,8,2560]{2,1,0:T(8,128)(2,1)}), bf16[128,8,2560]{2,1,0:T(8,128)(2,1)}, u32[]{:S(2)}, u32[]{:S(2)}) async-start(bf16[128,8,2560]{2,1,0:T(8,128)(2,1)} %fusion.2), calls=%async_computation.1 | async-start | bytes 10485760 | tf_op jit(solution)/shard_map/all_to_all | solution.py:101
  470.6 286.2 %reduce-scatter.4.cloned.1.call-start = ((), (), s32[]{:S(2)}) async-start(), calls=%async_computation.5 | async-start | bytes 819200
Sparse Core Ops, SparseCore 0:
  12.3 117.8 all-gather.2
  140.3 58.6 all-reduce.1
  691.5 65.1 reduce-scatter.3
where the time goes:
time: 766 us; the launch traced here: 765 us
  waiting for transfers between devices  433 us (57%)
  blocking collectives  253 us (33%)
  local copies, waits for them, and re-layouts  26.8 us (3%)
  other arithmetic  15.5 us (2%)
  between operations  13.9 us (2%)
  matrix products  12.3 us (2%)
  starting transfers between devices  9.73 us (1%)
    all_to_all x1, blocking collectives, on_device(): lax.all_to_all(doubled, 'req', split_axis=0, concat_axis=0, tiled=True)  253 us
    all_to_all x1, waiting for transfers between devices, on_device(): lax.all_to_all(partial_value.reshape(senders, items, width), 'req', split...  194 us
    all_gather x1, waiting for transfers between devices, on_device(): lax.all_gather(out_weight, 'req', axis=1, tiled=True)  118 us
    unnamed x4, waiting for transfers between devices  64.2 us
    psum x1, waiting for transfers between devices, on_device(): attn = lax.psum(attn_part, 'tp')  56.9 us
  transfers between devices with their start and end apart: 4, of which 4 were waited for; matrix products, arithmetic and copies ran while one was open for 1% of the time, Pallas kernels for 0%

commit v1 on v0

--- a/solution.py
+++ b/solution.py
@@ -1,3 +1,4 @@
+import functools
 import jax
 import jax.numpy as jnp
 from jax import lax
@@ -6,6 +7,20 @@
 HEAD_DIM = 128
 PAGE = 16
 epsilon = 1e-05
+
+
+def work_page_here(here_x, group_axis, row_dim):
+    piece_now = lax.all_to_all(
+        jnp.stack([here_x for _ in range(lax.axis_size(group_axis))]),
+        axis_name=group_axis,
+        split_axis=0,
+        concat_axis=0,
+    )
+    carry_out = jnp.concatenate(piece_now, axis=row_dim)
+    return carry_out
+
+
+unit_apply = functools.partial(work_page_here, group_axis="req", row_dim=1)
 
 
 def prompt_layout(lengths, count):
@@ -59,11 +74,7 @@
     own_start = lax.axis_index("tp") * share
     segment, offset = prompt_layout(lengths[0], count)
     context = attend(queries, key_values, segment)
-    attn_part = jnp.dot(
-        context,
-        lax.all_gather(out_weight, "req", axis=1, tiled=True),
-        preferred_element_type=jnp.float32,
-    )
+    attn_part = jnp.dot(context, unit_apply(out_weight), preferred_element_type=jnp.float32)
     attn = lax.psum(attn_part, "tp")
     mid_full = (hidden.astype(jnp.float32) + attn).astype(jnp.bfloat16)
     mid_wide = lax.optimization_barrier(mid_full).astype(jnp.float32)

time: 766 us -> 846 us (1.10)
  the two profiles are of different devices: /device:TPU:4 before, /device:TPU:2 now
where the time goes in v1:
time: 846 us; the launch traced here: 845 us
  waiting for transfers between devices  490 us (58%)
  blocking collectives  253 us (30%)
  starting transfers between devices  32.2 us (4%)
  local copies, waits for them, and re-layouts  28.3 us (3%)
  other arithmetic  14.9 us (2%)
  between operations  14.3 us (2%)
  matrix products  11.4 us (1%)
    all_to_all x1, blocking collectives, on_device(): lax.all_to_all(doubled, 'req', split_axis=0, concat_axis=0, tiled=True)  253 us
    all_to_all x1, waiting for transfers between devices, on_device(): lax.all_to_all(partial_value.reshape(senders, items, width), 'req', split...  204 us
    all_to_all x1, waiting for transfers between devices, work_page_here(): lax.all_to_all(jnp.stack([here_x for _ in range(lax.axis_size(group_axis)...  175 us
    psum x1, waiting for transfers between devices, on_device(): attn = lax.psum(attn_part, 'tp')  56.9 us
    unnamed x3, waiting for transfers between devices  54.1 us
    all_to_all x1, starting transfers between devices, work_page_here(): lax.all_to_all(jnp.stack([here_x for _ in range(lax.axis_size(group_axis)...  22.6 us
  transfers between devices with their start and end apart: 4, of which 4 were waited for; matrix products, arithmetic and copies ran while one was open for 1% of the time, Pallas kernels for 0%

profile of v1, /device:TPU:2, one launch (start us, length us, event | category | flops | bytes accessed | tf_op | source)
XLA Modules:
  0.0 844.7 jit_solution(18265635398694696123)
XLA Ops:
  7.2 0.0 copy-start
  7.2 0.0 copy-start.4
  7.2 0.0 copy-start.9
  7.2 0.0 copy-start.2
  7.2 3.1 stack.2
  10.3 22.6 %all-to-all-start = ((bf16[128,640,20]{1,2,0:T(8,128)(2,1)}), bf16[128,640,20]{1,2,0:T(8,128)(2,1)}, u32[]{:S(2)}, u32[]{:S(2)}) async-start(bf16[128,640,20]{1,2,0:T(8,128)(2,1)} %stack.2), calls=%async_computation | async-start | bytes 7864320 | tf_op jit(solution)/shard_map/all_to_all | solution.py:13
  32.9 0.0 all-reduce.2.cloned.1.call-start
  33.0 0.0 copy-done.4
  33.0 0.0 copy-done.9
  33.0 0.2 reduce-window.10
  33.2 0.1 convert_reduce_fusion.1
  33.3 0.1 fusion.30
  33.4 0.0 copy-done.2
  33.4 0.2 fusion.41
  33.7 0.2 fusion.7
  33.9 0.1 copy.58
  34.0 0.0 copy-done.3
  34.0 0.1 copy.59
  34.1 0.1 eq.88
  34.2 175.3 %all-to-all-done = bf16[128,640,20]{1,2,0:T(8,128)(2,1)} async-done(((bf16[128,640,20]{1,2,0:T(8,128)(2,1)}), bf16[128,640,20]{1,2,0:T(8,128)(2,1)}, u32[]{:S(2)}, u32[]{:S(2)}) %all-to-all-start) | async-done | bytes 3276832 | tf_op jit(solution)/shard_map/all_to_all | solution.py:13
  209.5 6.2 reshape.303
  215.7 3.9 fusion.22
  219.6 0.0 all-reduce.2.cloned.1.call-update
  219.6 0.1 reshape.304
  219.8 0.9 reduce-window.11
  220.7 0.2 slice_reduce_fusion
  220.9 0.1 fusion.20
  221.0 0.1 reduce_sum.93
  221.2 0.1 copy.62
  221.3 0.1 fusion.11
  221.4 56.9 %all-reduce.2.cloned.1.call-done = f32[64,2560]{1,0:T(8,128)} async-done(((f32[64,2560]{1,0:T(8,128)}), f32[64,2560]{1,0:T(8,128)}) %all-reduce.2.cloned.1.call-update) | async-done | bytes 655376 | tf_op jit(solution)/shard_map/psum | solution.py:78
  278.3 0.0 copy-done.1
  278.3 1.1 add_convert_fusion
  279.5 0.2 multiply_reduce_fusion.1
  279.6 0.0 copy-done.5
  279.6 0.9 fusion.3
  280.6 0.4 broadcast_in_dim.85
  281.0 253.4 %all_to_all.15 = bf16[128,8,2560]{2,1,0:T(8,128)(2,1)S(1)} all-to-all(bf16[128,8,2560]{2,1,0:T(8,128)(2,1)S(1)} %bitcast.109), channel_id=1, replica_groups=mesh['req'=128,'tp'=4] {'req'}, dimensions={0} | all-to-all | bytes 10485760 | tf_op jit(solution)/shard_map/all_to_all | solution.py:102
  534.4 0.0 copy-done
  534.4 2.2 fusion
  536.6 0.0 copy-done.8
  536.6 3.9 fusion.2
  540.6 9.5 %all-to-all-start.2 = ((bf16[128,8,2560]{2,1,0:T(8,128)(2,1)}), bf16[128,8,2560]{2,1,0:T(8,128)(2,1)}, u32[]{:S(2)}, u32[]{:S(2)}) async-start(bf16[128,8,2560]{2,1,0:T(8,128)(2,1)} %fusion.2), calls=%async_computation.2 | async-start | bytes 10485760 | tf_op jit(solution)/shard_map/all_to_all | solution.py:112
  550.1 0.0 reduce-scatter.4.cloned.1.call-start
  550.2 0.1 copy.64
  550.3 0.1 mul.113
  550.4 0.1 copy.63
  550.5 0.1 copy.65
  550.6 0.0 copy-done.7
  550.6 0.1 copy.66
  550.7 0.1 broadcast_in_dim.91
  550.9 203.9 %all-to-all-done.2 = bf16[128,8,2560]{2,1,0:T(8,128)(2,1)} async-done(((bf16[128,8,2560]{2,1,0:T(8,128)(2,1)}), bf16[128,8,2560]{2,1,0:T(8,128)(2,1)}, u32[]{:S(2)}, u32[]{:S(2)}) %all-to-all-start.2) | async-done | bytes 5242912 | tf_op jit(solution)/shard_map/all_to_all | solution.py:112
  754.8 6.2 convert_reduce_fusion
  761.0 8.4 gather_fusion
  769.4 5.1 gather.7
  774.5 4.7 multiply_reduce_fusion
  779.3 1.1 copy.68
  780.4 0.0 reduce-scatter.4.cloned.1.call-update
  780.4 0.1 select_reduce_fusion.1
  780.5 0.1 select_reduce_fusion
  780.6 1.4 scatter_custom_fusion
  782.0 54.1 %reduce-scatter.4.cloned.1.call-done = bf16[640,64]{1,0:T(8,128)(2,1)} async-done(((bf16[2560,64]{1,0:T(8,128)(2,1)}), bf16[640,64]{1,0:T(8,128)(2,1)}) %reduce-scatter.4.cloned.1.call-update) | async-done | bytes 81936
  836.1 1.0 copy.69
  837.2 0.7 add_convert_fusion.1
  (21 shorter events, 0.3 us)
Async XLA Ops:
  7.2 527.2 %copy-start = (bf16[1,2560,384]{2,1,0:T(8,128)(2,1)S(1)}, bf16[1,2560,384]{2,1,0:T(8,128)(2,1)}, u32[]{:S(2)}) copy-start(bf16[1,2560,384]{2,1,0:T(8,128)(2,1)} %param.20) | copy-start | bytes 5898244
  7.2 25.8 %copy-start.4 = (bf16[64,256]{1,0:T(8,128)(2,1)S(1)}, bf16[64,256]{1,0:T(8,128)(2,1)}, u32[]{:S(2)}) copy-start(bf16[64,256]{1,0:T(8,128)(2,1)} %param.12) | copy-start | bytes 98308
  7.2 25.8 %copy-start.9 = (s32[1,4]{1,0:T(1,128)S(1)}, s32[1,4]{1,0:T(1,128)}, u32[]{:S(2)}) copy-start(s32[1,4]{1,0:T(1,128)} %param.14) | copy-start | bytes 52
  7.2 26.2 %copy-start.2 = (bf16[64,640]{1,0:T(8,128)(2,1)S(1)}, bf16[64,640]{1,0:T(8,128)(2,1)}, u32[]{:S(2)}) copy-start(bf16[64,640]{1,0:T(8,128)(2,1)} %param.11) | copy-start | bytes 245764
  10.3 23.7 %copy-start.3 = (s32[64,6]{0,1:T(8,128)S(1)}, s32[64,6]{0,1:T(8,128)}, u32[]{:S(2)}) copy-start(s32[64,6]{0,1:T(8,128)} %param.18) | copy-start | bytes 4612
  10.3 199.2 %all-to-all-start = ((bf16[128,640,20]{1,2,0:T(8,128)(2,1)}), bf16[128,640,20]{1,2,0:T(8,128)(2,1)}, u32[]{:S(2)}, u32[]{:S(2)}) async-start(bf16[128,640,20]{1,2,0:T(8,128)(2,1)} %stack.2), calls=%async_computation | async-start | bytes 7864320 | tf_op jit(solution)/shard_map/all_to_all | solution.py:13
  32.9 245.4 %all-reduce.2.cloned.1.call-start = ((), (), s32[]{:S(2)}) async-start(), calls=%async_computation.4 | async-start | bytes 1310720 | tf_op jit(solution)/shard_map/psum | solution.py:78
  209.5 68.8 %copy-start.1 = (bf16[64,2560]{1,0:T(8,128)(2,1)S(1)}, bf16[64,2560]{1,0:T(8,128)(2,1)}, u32[]{:S(2)}) copy-start(bf16[64,2560]{1,0:T(8,128)(2,1)} %param.13) | copy-start | bytes 983044
  215.7 63.9 %copy-start.5 = (f32[2560]{0:T(1024)S(1)}, f32[2560]{0:T(1024)}, u32[]{:S(2)}) copy-start(f32[2560]{0:T(1024)} %param.17) | copy-start | bytes 30724
  534.4 2.2 copy-start.8
  540.6 9.9 %copy-start.6 = (f32[64,6]{0,1:T(8,128)S(1)}, f32[64,6]{0,1:T(8,128)}, u32[]{:S(2)}) copy-start(f32[64,6]{0,1:T(8,128)} %param.19) | copy-start | bytes 4612
  540.6 10.0 %copy-start.7 = (s32[1,4,2]{1,2,0:T(2,128)S(1)}, s32[1,4,2]{1,2,0:T(2,128)}, u32[]{:S(2)}) copy-start(s32[1,4,2]{1,2,0:T(2,128)} %param.15) | copy-start | bytes 100
  540.6 214.2 %all-to-all-start.2 = ((bf16[128,8,2560]{2,1,0:T(8,128)(2,1)}), bf16[128,8,2560]{2,1,0:T(8,128)(2,1)}, u32[]{:S(2)}, u32[]{:S(2)}) async-start(bf16[128,8,2560]{2,1,0:T(8,128)(2,1)} %fusion.2), calls=%async_computation.2 | async-start | bytes 10485760 | tf_op jit(solution)/shard_map/all_to_all | solution.py:112
  550.1 286.0 %reduce-scatter.4.cloned.1.call-start = ((), (), s32[]{:S(2)}) async-start(), calls=%async_computation.5 | async-start | bytes 819200
Sparse Core Ops, SparseCore 0:
  219.7 58.5 all-reduce.1
  780.5 55.5 reduce-scatter.3
